TPU v7x, 32 devices: a whole 2x2x4 slice. The times are simulated.
32 devices in a mesh: groups: 2 (over y), space: 4 (over z), ckpt: 2 (over x), rep: 2 (over core).
Axes of the slice: x: 2, y: 2, z: 4, core: 2. Of those that a mesh axis runs over, the one named last changes fastest.
Arguments:
- adj_disp: bfloat16 [320, 96, 768], P(('groups', 'space', 'rep'), None, 'ckpt'), parts along dimension 0, may hold values from -6 to 6
- adj_vel: bfloat16 [320, 96, 768], P(('groups', 'space', 'rep'), None, 'ckpt'), parts along dimension 0, may hold values from -6 to 6
- tangent_blocks: bfloat16 [320, 96, 768], P(('groups', 'space', 'rep')), parts along dimension 0, may hold values from -0.21875 to 0.21875
- block_cols: int32 [320, 8], P(('groups', 'space', 'rep')), parts along dimension 0, may hold values from 0 to 159, as said below
- inv_mass: float32 [320, 96], P(('groups', 'space', 'rep')), parts along dimension 0, may hold values from 0.25 to 1
- joint_stiff: float32 [320, 96], P(('groups', 'space', 'rep')), parts along dimension 0, may hold values from 0.2 to 1
- contact: int32 [3, 320], P(None, ('groups', 'space', 'rep')), parts along dimension 1, may hold values 0 or 1
- states: float32 [3, 320, 96], P(None, ('groups', 'space', 'rep'), 'ckpt'), parts along dimension 1, may hold values from -4 to 4
Outputs:
- disp_out: float32 [320, 96, 768], P(('groups', 'space', 'rep'), None, 'ckpt'), parts along dimension 0
- vel_out: float32 [320, 96, 768], P(('groups', 'space', 'rep'), None, 'ckpt'), parts along dimension 0
There are 2 independent parts, one for each index of `groups`. A program takes and returns all parts, laid end to end along the dimension named above; each array names one. Nothing has to cross between parts.
Inputs may be any that keep to these rules, and one draw needn't show every extreme that they name: `block_cols`: every block column lies within 4 block rows of its own block row, counted cyclically over the 160 block rows; each block row lists itself and the rows exactly 4 before and after it.
All inputs are finite; a program needn't handle non-finite values. No bound on the sum of `contact` on one device may be relied on, other than what follows from the above.
Results may differ from a plain program's by a relative error of at most 0.015.
Values may be sent and summed in bfloat16 or wider, within the bound.
No kernel may reach another device: no remote copies, remote signals or barrier semaphores. Data moves between devices by JAX's collectives and lax.ppermute only.
A program may use at most 128 MiB of HBM per device.

v0:
```python
import jax
import jax.numpy as jnp
from jax import lax
from jax.sharding import PartitionSpec as P

HB = 4
WINDOW = 3


def passed_along(array, axis, by):
    length = lax.axis_size(axis)
    return lax.ppermute(array, axis, [(i, (i + by) % length) for i in range(length)])


def body(adj_disp, adj_vel, tangent_blocks, block_cols, inv_mass, joint_stiff, contact, states):
    rows = tangent_blocks.shape[0]
    width = tangent_blocks.shape[1]
    slots = block_cols.shape[1]
    total_rows = rows * lax.axis_size(("space", "rep"))
    first = lax.axis_index(("space", "rep")) * rows
    local = jnp.arange(rows, dtype=jnp.int32)
    offset = jnp.mod(block_cols - (first + local)[:, None] + HB, total_rows) - HB
    position = local[:, None] + HB + offset
    disp = adj_disp.astype(jnp.float32)
    vel = adj_vel.astype(jnp.float32)
    accel = jnp.zeros(disp.shape, jnp.float32)
    for back in range(WINDOW):
        step = WINDOW - 1 - back
        state_now = lax.all_gather(states[step], "ckpt", axis=1, tiled=True)
        total = accel + 0.5 * vel
        packed = (inv_mass[:, :, None] * total).astype(jnp.bfloat16)
        coeff = (
            3.0 * joint_stiff * contact[step].astype(jnp.float32)[:, None] * state_now * state_now
        )
        lower = passed_along(packed[rows - HB :], ("space", "rep"), 1)
        upper = passed_along(packed[:HB], ("space", "rep"), -1)
        extended = jnp.concatenate([lower, packed, upper], axis=0)
        picked = extended[position].reshape(rows, slots * width, packed.shape[2])
        product = jnp.einsum(
            "bik,bkr->bir", tangent_blocks, picked, preferred_element_type=jnp.float32
        )
        image = product + coeff[:, :, None] * packed.astype(jnp.float32)
        disp = disp - image
        accel = 0.5 * disp + 0.5 * vel
        vel = vel + disp
    return (disp, vel)


def solution(mesh):
    placed = (
        P(("groups", "space", "rep"), None, "ckpt"),
        P(("groups", "space", "rep"), None, "ckpt"),
        P(("groups", "space", "rep"), None, None),
        P(("groups", "space", "rep"), None),
        P(("groups", "space", "rep"), None),
        P(("groups", "space", "rep"), None),
        P(None, ("groups", "space", "rep")),
        P(None, ("groups", "space", "rep"), "ckpt"),
    )
    return jax.shard_map(
        body,
        mesh=mesh,
        in_specs=placed,
        out_specs=(
            P(("groups", "space", "rep"), None, "ckpt"),
            P(("groups", "space", "rep"), None, "ckpt"),
        ),
        check_vma=False,
    )
```

profile of v0, /device:TPU:0, one launch (start us, length us, event | category | flops | bytes accessed | tf_op | source)
XLA Modules:
  0.0 129.3 jit_solution(14847695931026815950)
XLA Ops:
  1.5 1.7 %fusion = bf16[20,96,384]{2,1,0:T(8,128)(2,1)S(1)} fusion(bf16[20,96,384]{2,1,0:T(8,128)(2,1)} %param.9, f32[20,96]{1,0:T(8,128)S(1)} %broadcast_multiply_fusion), kind=kLoop, calls=%fused_computation.5 | loop fusion | flops 2211840 | bytes 2956800 | tf_op jit(solution)/shard_map/convert_element_type | solution.py:31
  5.7 4.0 %collective-permute-start.1 = (bf16[4,96,384]{2,1,0:T(8,128)(2,1)}, bf16[4,96,384]{2,1,0:T(8,128)(2,1)S(1)}, u32[]{:S(2)}, u32[]{:S(2)}) collective-permute-start(bf16[4,96,384]{2,1,0:T(8,128)(2,1)} %get-tuple-element.7), channel_id=1, source_target_pairs={{0,13},{1,0},{4,1},{5,4},{8,5},{9,8},{12,9},{13,12},{2,15},{3,2},{... | collective-permute-start | bytes 884744 | tf_op jit(solution)/shard_map/ppermute | solution.py:12
  14.5 1.4 %copy.30 = f32[1,20,48]{1,0,2:T(1,128)} copy(f32[1,20,48]{2,1,0:T(8,128)} %get-tuple-element.8) | data formatting | bytes 7680
  15.9 6.1 %all-gather.2 = f32[1,20,96]{1,0,2:T(1,128)} all-gather(f32[1,20,48]{1,0,2:T(1,128)} %copy.30), channel_id=4, replica_groups=mesh['groups'=2,'space'=4,'ckpt'=2,'rep'=2] {'ckpt'}, dimensions={2}, use_global_device_ids=true | all-gather | bytes 11520 | tf_op jit(solution)/shard_map/all_gather | solution.py:29
  21.9 1.5 %copy.27 = f32[1,20,96]{2,1,0:T(8,128)} copy(f32[1,20,96]{1,0,2:T(1,128)} %all-gather.2) | data formatting | bytes 15360 | tf_op jit(solution)/shard_map/all_gather | solution.py:29
  24.8 4.8 %all-gather.1 = f32[1,20,96]{1,0,2:T(1,128)} all-gather(f32[1,20,48]{1,0,2:T(1,128)} %copy.29), channel_id=3, replica_groups=mesh['groups'=2,'space'=4,'ckpt'=2,'rep'=2] {'ckpt'}, dimensions={2}, use_global_device_ids=true | all-gather | bytes 11520 | tf_op jit(solution)/shard_map/all_gather | solution.py:29
  29.6 1.5 %copy.25 = f32[1,20,96]{2,1,0:T(8,128)} copy(f32[1,20,96]{1,0,2:T(1,128)} %all-gather.1) | data formatting | bytes 15360 | tf_op jit(solution)/shard_map/all_gather | solution.py:29
  31.1 1.4 %copy.28 = f32[1,20,48]{1,0,2:T(1,128)} copy(f32[1,20,48]{2,1,0:T(8,128)} %get-tuple-element.10) | data formatting | bytes 7680
  32.5 5.4 %all-gather = f32[1,20,96]{1,0,2:T(1,128)} all-gather(f32[1,20,48]{1,0,2:T(1,128)} %copy.28), channel_id=2, replica_groups=mesh['groups'=2,'space'=4,'ckpt'=2,'rep'=2] {'ckpt'}, dimensions={2}, use_global_device_ids=true | all-gather | bytes 11520 | tf_op jit(solution)/shard_map/all_gather | solution.py:29
  37.9 1.5 %copy.23 = f32[1,20,96]{2,1,0:T(8,128)} copy(f32[1,20,96]{1,0,2:T(1,128)} %all-gather) | data formatting | bytes 15360 | tf_op jit(solution)/shard_map/all_gather | solution.py:29
  40.0 1.5 %multiply_multiply_fusion = (f32[20,96]{1,0:T(8,128)}, f32[20,96]{1,0:T(8,128)}, f32[20,96]{1,0:T(8,128)}) fusion(f32[1,20,96]{2,1,0:T(8,128)} %copy.27, f32[20,96]{1,0:T(8,128)} %param.13, f32[20]{0:T(128)} %get-tuple-element.14, f32[1,20,96]{2,1,0:T(8,128)} %copy.23, f32[20]{0:T(128)} %get-tuple-element.15, f32[1,20,96]{2,1,0:T(8,128)} %copy.25, ...), kind=kLoop, calls=%fused_computation.19 | loop fusion | flops 17280 | bytes 54000 | tf_op jit(solution)/shard_map/mul | solution.py:33
  41.5 3.0 %pad_maximum_fusion = bf16[28,96,384]{2,1,0:T(8,128)(2,1)} fusion(bf16[4,96,384]{2,1,0:T(8,128)(2,1)S(1)} %collective-permute-done.1, bf16[20,96,384]{2,1,0:T(8,128)(2,1)} %copy-done.3, bf16[4,96,384]{2,1,0:T(8,128)(2,1)S(1)} %collective-permute-done), kind=kLoop, calls=%fused_computation.14 | loop fusion | flops 2064384 | bytes 4128768 | tf_op jit(solution)/shard_map/concatenate | solution.py:37
  44.5 10.3 %gather_fusion = bf16[160,96,384]{2,1,0:T(8,128)(2,1)} fusion(bf16[28,96,384]{2,1,0:T(8,128)(2,1)} %pad_maximum_fusion, s32[1024]{0:T(1024)S(1)} %pad_clamp_fusion), kind=kCustom, calls=%fused_computation | custom fusion | bytes 23593600 | tf_op jit(solution)/shard_map/gather | solution.py:38
  54.8 7.6 %multiply_convert_fusion.1 = (bf16[20,96,384]{2,1,0:T(8,128)(2,1)S(1)}, f32[20,96,384]{2,1,0:T(8,128)}) fusion(f32[20,96]{1,0:T(8,128)S(1)} %copy-done.4, bf16[20,96,384]{2,1,0:T(8,128)(2,1)} %param.9, f32[20,96]{1,0:T(8,128)S(1)} %copy-done.6, bf16[20,96,768]{2,1,0:T(8,128)(2,1)S(1)} %copy-done, bf16[20,768,384]{2,1,0:T(8,128)(2,1)} %bitcast.34, ...), kind=kOutput, calls=%fused_computation.13 | convolution fusion | flops 1142046720 | bytes 22141440 | tf_op jit(solution)/shard_map/bik,bkr->bir/dot_general | solution.py:39
  62.5 3.5 %collective-permute-start.3 = (bf16[4,96,384]{2,1,0:T(8,128)(2,1)S(1)}, bf16[4,96,384]{2,1,0:T(8,128)(2,1)S(1)}, u32[]{:S(2)}, u32[]{:S(2)}) collective-permute-start(bf16[4,96,384]{2,1,0:T(8,128)(2,1)S(1)} %get-tuple-element.5), channel_id=1, source_target_pairs={{0,13},{1,0},{4,1},{5,4},{8,5},{9,8},{12,9},{13,12},{2,15},{3,2},{... | collective-permute-start | bytes 884744 | tf_op jit(solution)/shard_map/ppermute | solution.py:12
  66.0 7.3 %collective-permute-done.2 = bf16[4,96,384]{2,1,0:T(8,128)(2,1)S(1)} collective-permute-done((bf16[4,96,384]{2,1,0:T(8,128)(2,1)S(1)}, bf16[4,96,384]{2,1,0:T(8,128)(2,1)S(1)}, u32[]{:S(2)}, u32[]{:S(2)}) %collective-permute-start.2) | collective-permute-done | bytes 294944 | tf_op jit(solution)/shard_map/ppermute | solution.py:12
  73.3 1.6 %pad_maximum_fusion.1 = bf16[28,96,384]{2,1,0:T(8,128)(2,1)} fusion(bf16[4,96,384]{2,1,0:T(8,128)(2,1)S(1)} %collective-permute-done.3, bf16[20,96,384]{2,1,0:T(8,128)(2,1)S(1)} %get-tuple-element.17, bf16[4,96,384]{2,1,0:T(8,128)(2,1)S(1)} %collective-permute-done.2), kind=kLoop, calls=%fused_computation.15 | loop fusion | flops 2064384 | bytes 4128768 | tf_op jit(solution)/shard_map/concatenate | solution.py:37
  74.9 10.3 %gather_fusion.1 = bf16[160,96,384]{2,1,0:T(8,128)(2,1)} fusion(bf16[28,96,384]{2,1,0:T(8,128)(2,1)} %pad_maximum_fusion.1, s32[1024]{0:T(1024)S(1)} %pad_clamp_fusion), kind=kCustom, calls=%fused_computation.1 | custom fusion | bytes 23593600 | tf_op jit(solution)/shard_map/gather | solution.py:38
  85.2 10.4 %multiply_convert_fusion = (bf16[20,96,384]{2,1,0:T(8,128)(2,1)S(1)}, f32[20,96,384]{2,1,0:T(8,128)}) fusion(f32[20,96]{1,0:T(8,128)S(1)} %copy-done.4, f32[20,96,384]{2,1,0:T(8,128)} %get-tuple-element.18, bf16[20,96,384]{2,1,0:T(8,128)(2,1)} %param.9, bf16[20,96,384]{2,1,0:T(8,128)(2,1)} %copy-done.1, f32[20,96]{1,0:T(8,128)S(1)} %copy-done.5, ...), kind=kOutput, calls=%fused_computation.12 | convolution fusion | flops 1142784000 | bytes 25082880 | tf_op jit(solution)/shard_map/bik,bkr->bir/dot_general | solution.py:39
  95.7 3.5 %collective-permute-start.5 = (bf16[4,96,384]{2,1,0:T(8,128)(2,1)S(1)}, bf16[4,96,384]{2,1,0:T(8,128)(2,1)S(1)}, u32[]{:S(2)}, u32[]{:S(2)}) collective-permute-start(bf16[4,96,384]{2,1,0:T(8,128)(2,1)S(1)} %get-tuple-element.3), channel_id=1, source_target_pairs={{0,13},{1,0},{4,1},{5,4},{8,5},{9,8},{12,9},{13,12},{2,15},{3,2},{... | collective-permute-start | bytes 884744 | tf_op jit(solution)/shard_map/ppermute | solution.py:12
  99.2 6.3 %collective-permute-done.4 = bf16[4,96,384]{2,1,0:T(8,128)(2,1)S(1)} collective-permute-done((bf16[4,96,384]{2,1,0:T(8,128)(2,1)S(1)}, bf16[4,96,384]{2,1,0:T(8,128)(2,1)S(1)}, u32[]{:S(2)}, u32[]{:S(2)}) %collective-permute-start.4) | collective-permute-done | bytes 294944 | tf_op jit(solution)/shard_map/ppermute | solution.py:12
  105.5 1.7 %pad_maximum_fusion.2 = bf16[28,96,384]{2,1,0:T(8,128)(2,1)} fusion(bf16[4,96,384]{2,1,0:T(8,128)(2,1)S(1)} %collective-permute-done.5, bf16[20,96,384]{2,1,0:T(8,128)(2,1)S(1)} %get-tuple-element.19, bf16[4,96,384]{2,1,0:T(8,128)(2,1)S(1)} %collective-permute-done.4), kind=kLoop, calls=%fused_computation.16 | loop fusion | flops 2064384 | bytes 4128768 | tf_op jit(solution)/shard_map/concatenate | solution.py:37
  107.2 10.3 %gather_fusion.2 = bf16[160,96,384]{2,1,0:T(8,128)(2,1)} fusion(bf16[28,96,384]{2,1,0:T(8,128)(2,1)} %pad_maximum_fusion.2, s32[1024]{0:T(1024)S(1)} %pad_clamp_fusion), kind=kCustom, calls=%fused_computation.2 | custom fusion | bytes 23593600 | tf_op jit(solution)/shard_map/gather | solution.py:38
  117.5 11.8 %fusion.5 = (f32[20,96,384]{2,1,0:T(8,128)}, f32[20,96,384]{2,1,0:T(8,128)}) fusion(f32[20,96,384]{2,1,0:T(8,128)} %get-tuple-element.20, f32[20,96,384]{2,1,0:T(8,128)} %get-tuple-element.18, bf16[20,96,384]{2,1,0:T(8,128)(2,1)} %param.9, bf16[20,96,384]{2,1,0:T(8,128)(2,1)} %copy-done.2, f32[20,96]{1,0:T(8,128)S(1)} %copy-done.7, ...), kind=kOutput, calls=%fused_computation.18 | convolution fusion | flops 1138360320 | bytes 29498880 | tf_op jit(solution)/shard_map/bik,bkr->bir/dot_general | solution.py:39
  (37 shorter events, 10.4 us)
Async XLA Ops:
  0.6 54.2 %copy-start = (bf16[20,96,768]{2,1,0:T(8,128)(2,1)S(1)}, bf16[20,96,768]{2,1,0:T(8,128)(2,1)}, u32[]{:S(2)}) copy-start(bf16[20,96,768]{2,1,0:T(8,128)(2,1)} %param.10) | copy-start | bytes 8847364
  0.6 9.1 %copy-start.8 = (s32[3,20]{1,0:T(4,128)S(1)}, s32[3,20]{1,0:T(4,128)}, u32[]{:S(2)}) copy-start(s32[3,20]{1,0:T(4,128)} %param.14) | copy-start | bytes 724
  3.3 1.1 copy-start.3
  5.2 36.2 %collective-permute-start = (bf16[4,96,384]{2,1,0:T(8,128)(2,1)}, bf16[4,96,384]{2,1,0:T(8,128)(2,1)S(1)}, u32[]{:S(2)}, u32[]{:S(2)}) collective-permute-start(bf16[4,96,384]{2,1,0:T(8,128)(2,1)} %get-tuple-element.6), channel_id=1, source_target_pairs={{0,1},{1,4},{4,5},{5,8},{8,9},{9,12},{12,13},{13,0},{2,3},{3,6},{6... | collective-permute-start | bytes 884744 | tf_op jit(solution)/shard_map/ppermute | solution.py:12
  5.7 35.8 %collective-permute-start.1 = (bf16[4,96,384]{2,1,0:T(8,128)(2,1)}, bf16[4,96,384]{2,1,0:T(8,128)(2,1)S(1)}, u32[]{:S(2)}, u32[]{:S(2)}) collective-permute-start(bf16[4,96,384]{2,1,0:T(8,128)(2,1)} %get-tuple-element.7), channel_id=1, source_target_pairs={{0,13},{1,0},{4,1},{5,4},{8,5},{9,8},{12,9},{13,12},{2,15},{3,2},{... | collective-permute-start | bytes 884744 | tf_op jit(solution)/shard_map/ppermute | solution.py:12
  44.5 10.3 %copy-start.4 = (f32[20,96]{1,0:T(8,128)S(1)}, f32[20,96]{1,0:T(8,128)}, u32[]{:S(2)}) copy-start(f32[20,96]{1,0:T(8,128)} %param.12) | copy-start | bytes 23044
  44.5 10.3 %copy-start.6 = (f32[20,96]{1,0:T(8,128)S(1)}, f32[20,96]{1,0:T(8,128)}, u32[]{:S(2)}) copy-start(f32[20,96]{1,0:T(8,128)} %get-tuple-element.12) | copy-start | bytes 23044
  62.3 10.9 %copy-start.1 = (bf16[20,96,384]{2,1,0:T(8,128)(2,1)}, bf16[20,96,384]{2,1,0:T(8,128)(2,1)S(1)}, u32[]{:S(2)}) copy-start(bf16[20,96,384]{2,1,0:T(8,128)(2,1)S(1)} %get-tuple-element.17) | copy-start | bytes 4423684
  62.4 10.9 %collective-permute-start.2 = (bf16[4,96,384]{2,1,0:T(8,128)(2,1)S(1)}, bf16[4,96,384]{2,1,0:T(8,128)(2,1)S(1)}, u32[]{:S(2)}, u32[]{:S(2)}) collective-permute-start(bf16[4,96,384]{2,1,0:T(8,128)(2,1)S(1)} %get-tuple-element.4), channel_id=1, source_target_pairs={{0,1},{1,4},{4,5},{5,8},{8,9},{9,12},{12,13},{13,0},{2,3},{3,6},{6... | collective-permute-start | bytes 884744 | tf_op jit(solution)/shard_map/ppermute | solution.py:12
  62.5 10.8 %collective-permute-start.3 = (bf16[4,96,384]{2,1,0:T(8,128)(2,1)S(1)}, bf16[4,96,384]{2,1,0:T(8,128)(2,1)S(1)}, u32[]{:S(2)}, u32[]{:S(2)}) collective-permute-start(bf16[4,96,384]{2,1,0:T(8,128)(2,1)S(1)} %get-tuple-element.5), channel_id=1, source_target_pairs={{0,13},{1,0},{4,1},{5,4},{8,5},{9,8},{12,9},{13,12},{2,15},{3,2},{... | collective-permute-start | bytes 884744 | tf_op jit(solution)/shard_map/ppermute | solution.py:12
  74.9 10.3 %copy-start.5 = (f32[20,96]{1,0:T(8,128)S(1)}, f32[20,96]{1,0:T(8,128)}, u32[]{:S(2)}) copy-start(f32[20,96]{1,0:T(8,128)} %get-tuple-element.13) | copy-start | bytes 23044
  95.6 10.0 %copy-start.2 = (bf16[20,96,384]{2,1,0:T(8,128)(2,1)}, bf16[20,96,384]{2,1,0:T(8,128)(2,1)S(1)}, u32[]{:S(2)}) copy-start(bf16[20,96,384]{2,1,0:T(8,128)(2,1)S(1)} %get-tuple-element.19) | copy-start | bytes 4423684
  95.6 9.9 %collective-permute-start.4 = (bf16[4,96,384]{2,1,0:T(8,128)(2,1)S(1)}, bf16[4,96,384]{2,1,0:T(8,128)(2,1)S(1)}, u32[]{:S(2)}, u32[]{:S(2)}) collective-permute-start(bf16[4,96,384]{2,1,0:T(8,128)(2,1)S(1)} %get-tuple-element.2), channel_id=1, source_target_pairs={{0,1},{1,4},{4,5},{5,8},{8,9},{9,12},{12,13},{13,0},{2,3},{3,6},{6... | collective-permute-start | bytes 884744 | tf_op jit(solution)/shard_map/ppermute | solution.py:12
  95.7 9.8 %collective-permute-start.5 = (bf16[4,96,384]{2,1,0:T(8,128)(2,1)S(1)}, bf16[4,96,384]{2,1,0:T(8,128)(2,1)S(1)}, u32[]{:S(2)}, u32[]{:S(2)}) collective-permute-start(bf16[4,96,384]{2,1,0:T(8,128)(2,1)S(1)} %get-tuple-element.3), channel_id=1, source_target_pairs={{0,13},{1,0},{4,1},{5,4},{8,5},{9,8},{12,9},{13,12},{2,15},{3,2},{... | collective-permute-start | bytes 884744 | tf_op jit(solution)/shard_map/ppermute | solution.py:12
  107.2 10.3 %copy-start.7 = (f32[20,96]{1,0:T(8,128)S(1)}, f32[20,96]{1,0:T(8,128)}, u32[]{:S(2)}) copy-start(f32[20,96]{1,0:T(8,128)} %get-tuple-element.11) | copy-start | bytes 23044
where the time goes:
time: 130 us; the launch traced here: 129 us
  local copies, waits for them, and re-layouts  45 us (35%)
  matrix products  29.8 us (23%)
  blocking collectives  16.3 us (13%)
  waiting for transfers between devices  13.6 us (10%)
  other arithmetic  12.3 us (9%)
  starting transfers between devices  11.7 us (9%)
    gather x3, local copies, waits for them, and re-layouts, body(): picked = extended[position].reshape(rows, slots * width, packed.shape[2])  30.9 us
    dot_general x3, matrix products, body(): jnp.einsum('bik,bkr->bir', tangent_blocks, picked, preferred_element_type...  29.8 us
    all_gather x3, blocking collectives, body(): state_now = lax.all_gather(states[step], 'ckpt', axis=1, tiled=True)  16.3 us
    ppermute x6, waiting for transfers between devices, passed_along(): lax.ppermute(array, axis, [(i, (i + by) % length) for i in range(length)])  13.6 us
    ppermute x6, starting transfers between devices, passed_along(): lax.ppermute(array, axis, [(i, (i + by) % length) for i in range(length)])  11.7 us
    concatenate x3, other arithmetic, body(): extended = jnp.concatenate([lower, packed, upper], axis=0)  6.24 us
    unnamed x21, local copies, waits for them, and re-layouts  5.3 us
    all_gather x3, local copies, waits for them, and re-layouts, body(): state_now = lax.all_gather(states[step], 'ckpt', axis=1, tiled=True)  4.42 us
  transfers between devices with their start and end apart: 6, of which 2 were waited for; matrix products, arithmetic and copies ran while one was open for 12% of the time, Pallas kernels for 0%

commit v1 on v0

--- a/solution.py
+++ b/solution.py
@@ -5,6 +5,27 @@
 
 HB = 4
 WINDOW = 3
+
+
+def lead_circles(m, dim_no):
+    m = jnp.moveaxis(m, 0, dim_no)
+    later = m.shape
+    return m.reshape(*later[:dim_no], later[dim_no] * later[dim_no + 1], *later[dim_no + 2 :])
+
+
+def clear_point_up(local_x, axis_key):
+    main, block_now = (lax.axis_size(axis_key), lax.axis_index(axis_key))
+    v_next, y2 = (local_x[None], 1)
+    while y2 < main:
+        r1 = lax.ppermute(
+            v_next, axis_key, list(map(lambda src_i: (src_i, src_i ^ y2), range(main)))
+        )
+        current_arr = block_now & y2 == 0
+        v_next = jnp.concatenate(
+            [jnp.where(current_arr, v_next, r1), jnp.where(current_arr, r1, v_next)]
+        )
+        y2 *= 2
+    return v_next
 
 
 def passed_along(array, axis, by):
@@ -26,7 +47,11 @@
     accel = jnp.zeros(disp.shape, jnp.float32)
     for back in range(WINDOW):
         step = WINDOW - 1 - back
-        state_now = lax.all_gather(states[step], "ckpt", axis=1, tiled=True)
+
+        def loops_draw(w_in, mine_x, row_dim):
+            return lead_circles(clear_point_up(w_in, mine_x), row_dim)
+
+        state_now = loops_draw(states[step], "ckpt", 1)
         total = accel + 0.5 * vel
         packed = (inv_mass[:, :, None] * total).astype(jnp.bfloat16)
         coeff = (

time: 130 us -> 119 us (0.915)
  blocking collectives: 16.3 us -> 0 us
  starting transfers between devices: 11.7 us -> 15.7 us
  other arithmetic: 12.3 us -> 14.8 us
  local copies, waits for them, and re-layouts: 45 us -> 43.2 us
    all_gather x3 -> x0, blocking collectives: 16.3 us -> none  [body(): state_now = lax.all_gather(states[step], 'ckpt', axis=1, tiled=True)]
    ppermute x0 -> x3, starting transfers between devices: none -> 4.96 us  [clear_point_up(): lax.ppermute(v_next, axis_key, list(map(lambda src_i: (src_i, src_i ^ y2)...]
    all_gather x3 -> x0, local copies, waits for them, and re-layouts: 4.42 us -> none  [body(): state_now = lax.all_gather(states[step], 'ckpt', axis=1, tiled=True)]
    reshape x0 -> x3, local copies, waits for them, and re-layouts: none -> 4.21 us  [lead_circles(): m.reshape(*later[:dim_no], later[dim_no] * later[dim_no + 1], *later[dim_...]
    unnamed x21 -> x18, local copies, waits for them, and re-layouts: 5.3 us -> 1.14 us
    transpose x0 -> x3, local copies, waits for them, and re-layouts: none -> 2.56 us  [lead_circles(): m = jnp.moveaxis(m, 0, dim_no)]
    select_n x0 -> x2, other arithmetic: none -> 2.12 us  [clear_point_up(): jnp.where(current_arr, v_next, r1)]
  transfers between devices with their start and end apart: 6 -> 9, of which waited for: 2 -> 3; matrix products, arithmetic and copies ran while one was open for 12% -> 15% of each run, Pallas kernels for 0% -> 0%
where the time goes in v1:
time: 119 us; the launch traced here: 118 us
  local copies, waits for them, and re-layouts  43.2 us (36%)
  matrix products  29.8 us (25%)
  starting transfers between devices  15.7 us (13%)
  other arithmetic  14.8 us (12%)
  waiting for transfers between devices  13.7 us (12%)
    gather x3, local copies, waits for them, and re-layouts, body(): picked = extended[position].reshape(rows, slots * width, packed.shape[2])  30.8 us
    dot_general x3, matrix products, body(): jnp.einsum('bik,bkr->bir', tangent_blocks, picked, preferred_element_type...  29.8 us
    ppermute x6, waiting for transfers between devices, passed_along(): lax.ppermute(array, axis, [(i, (i + by) % length) for i in range(length)])  13.6 us
    ppermute x6, starting transfers between devices, passed_along(): lax.ppermute(array, axis, [(i, (i + by) % length) for i in range(length)])  10.7 us
    concatenate x3, other arithmetic, body(): extended = jnp.concatenate([lower, packed, upper], axis=0)  6.22 us
    ppermute x3, starting transfers between devices, clear_point_up(): lax.ppermute(v_next, axis_key, list(map(lambda src_i: (src_i, src_i ^ y2)...  4.96 us
    reshape x3, local copies, waits for them, and re-layouts, lead_circles(): m.reshape(*later[:dim_no], later[dim_no] * later[dim_no + 1], *later[dim_...  4.21 us
    transpose x3, local copies, waits for them, and re-layouts, lead_circles(): m = jnp.moveaxis(m, 0, dim_no)  2.56 us
  transfers between devices with their start and end apart: 9, of which 3 were waited for; matrix products, arithmetic and copies ran while one was open for 15% of the time, Pallas kernels for 0%

profile of v1, /device:TPU:0, one launch (start us, length us, event | category | flops | bytes accessed | tf_op | source)
XLA Modules:
  0.0 117.9 jit_solution(3998810670776794092)
XLA Ops:
  0.7 1.5 %slice.47 = f32[1,20,48]{2,1,0:T(8,128)} slice(f32[3,20,48]{2,1,0:T(8,128)} %param.15), slice={[0:1], [0:20], [0:48]} | slice | bytes 7680 | tf_op jit(solution)/shard_map/slice | solution.py:54
  2.1 2.9 %collective-permute-start.8 = (f32[1,20,48]{2,1,0:T(8,128)}, f32[1,20,48]{2,1,0:T(8,128)}, u32[]{:S(2)}, u32[]{:S(2)}) collective-permute-start(f32[1,20,48]{2,1,0:T(8,128)} %slice.47), channel_id=1, source_target_pairs={{0,2},{2,0},{1,3},{3,1},{4,6},{6,4},{5,7},{7,5},{8,10},{10,8},{9,1... | collective-permute-start | bytes 11528 | tf_op jit(solution)/shard_map/ppermute | solution.py:20
  5.8 1.7 %fusion = bf16[20,96,384]{2,1,0:T(8,128)(2,1)S(1)} fusion(bf16[20,96,384]{2,1,0:T(8,128)(2,1)} %param.9, f32[20,96]{1,0:T(8,128)S(1)} %broadcast_multiply_fusion), kind=kLoop, calls=%fused_computation.5 | loop fusion | flops 2211840 | bytes 2956800 | tf_op jit(solution)/shard_map/convert_element_type | solution.py:56
  9.5 3.5 %collective-permute-start.1 = (bf16[4,96,384]{2,1,0:T(8,128)(2,1)}, bf16[4,96,384]{2,1,0:T(8,128)(2,1)S(1)}, u32[]{:S(2)}, u32[]{:S(2)}) collective-permute-start(bf16[4,96,384]{2,1,0:T(8,128)(2,1)} %get-tuple-element.7), channel_id=1, source_target_pairs={{0,13},{1,0},{4,1},{5,4},{8,5},{9,8},{12,9},{13,12},{2,15},{3,2},{... | collective-permute-start | bytes 884744 | tf_op jit(solution)/shard_map/ppermute | solution.py:33
  15.0 1.4 %reshape.67 = s32[160]{0:T(256)} reshape(s32[20,8]{1,0:T(8,128)} %copy.10) | data formatting | bytes 1280 | tf_op jit(solution)/shard_map/broadcast_in_dim | solution.py:63
  17.0 1.4 %broadcast_select_fusion.1 = (f32[1,20,48]{2,1,0:T(8,128)S(1)}, f32[1,20,48]{2,1,0:T(8,128)S(1)}, f32[1,20,48]{2,1,0:T(8,128)}, f32[1,20,48]{2,1,0:T(8,128)}) fusion(f32[1,20,48]{2,1,0:T(8,128)} %collective-permute-done.8, pred[]{:T(512)S(6)} %eq.4, f32[3,20,48]{2,1,0:T(8,128)} %param.15), kind=kLoop, calls=%fused_computation.29 | loop fusion | flops 1920 | bytes 30721 | tf_op jit(solution)/shard_map/jit(_where)/select_n | solution.py:25
  18.4 2.0 %collective-permute-start.5 = (f32[1,20,48]{2,1,0:T(8,128)}, f32[1,20,48]{2,1,0:T(8,128)}, u32[]{:S(2)}, u32[]{:S(2)}) collective-permute-start(f32[1,20,48]{2,1,0:T(8,128)} %get-tuple-element.15), channel_id=1, source_target_pairs={{0,2},{2,0},{1,3},{3,1},{4,6},{6,4},{5,7},{7,5},{8,10},{10,8},{9,1... | collective-permute-start | bytes 11528 | tf_op jit(solution)/shard_map/ppermute | solution.py:20
  21.0 1.4 %reshape.64 = f32[20,96]{1,0:T(8,128)} reshape(f32[20,2,48]{2,1,0:T(2,128)} %copy.13) | data formatting | bytes 15360 | tf_op jit(solution)/shard_map/reshape | solution.py:13
  24.5 1.4 %reshape.60 = f32[20,96]{1,0:T(8,128)} reshape(f32[20,2,48]{2,1,0:T(2,128)} %copy.11) | data formatting | bytes 15360 | tf_op jit(solution)/shard_map/reshape | solution.py:13
  27.2 1.4 %reshape.62 = f32[20,96]{1,0:T(8,128)} reshape(f32[20,2,48]{2,1,0:T(2,128)} %copy.12) | data formatting | bytes 15360 | tf_op jit(solution)/shard_map/reshape | solution.py:13
  28.7 1.4 %multiply_multiply_fusion = (f32[20,96]{1,0:T(8,128)}, f32[20,96]{1,0:T(8,128)}, f32[20,96]{1,0:T(8,128)}) fusion(f32[20,96]{1,0:T(8,128)} %reshape.64, f32[20,96]{1,0:T(8,128)} %param.13, f32[20]{0:T(128)} %get-tuple-element.21, f32[20,96]{1,0:T(8,128)} %reshape.60, f32[20]{0:T(128)} %get-tuple-element.22, f32[20,96]{1,0:T(8,128)} %reshape.62, ...), kind=kLoop, calls=%fused_computation.22 | loop fusion | flops 17280 | bytes 54000 | tf_op jit(solution)/shard_map/mul | solution.py:58
  30.1 3.0 %pad_maximum_fusion = bf16[28,96,384]{2,1,0:T(8,128)(2,1)} fusion(bf16[4,96,384]{2,1,0:T(8,128)(2,1)S(1)} %collective-permute-done.1, bf16[20,96,384]{2,1,0:T(8,128)(2,1)} %copy-done.3, bf16[4,96,384]{2,1,0:T(8,128)(2,1)S(1)} %collective-permute-done), kind=kLoop, calls=%fused_computation.14 | loop fusion | flops 2064384 | bytes 4128768 | tf_op jit(solution)/shard_map/concatenate | solution.py:62
  33.1 10.3 %gather_fusion = bf16[160,96,384]{2,1,0:T(8,128)(2,1)} fusion(bf16[28,96,384]{2,1,0:T(8,128)(2,1)} %pad_maximum_fusion, s32[1024]{0:T(1024)S(1)} %pad_clamp_fusion), kind=kCustom, calls=%fused_computation | custom fusion | bytes 23593600 | tf_op jit(solution)/shard_map/gather | solution.py:63
  43.4 7.6 %multiply_convert_fusion.1 = (bf16[20,96,384]{2,1,0:T(8,128)(2,1)S(1)}, f32[20,96,384]{2,1,0:T(8,128)}) fusion(f32[20,96]{1,0:T(8,128)S(1)} %copy-done.4, bf16[20,96,384]{2,1,0:T(8,128)(2,1)} %param.9, f32[20,96]{1,0:T(8,128)S(1)} %copy-done.6, bf16[20,96,768]{2,1,0:T(8,128)(2,1)S(1)} %copy-done, bf16[20,768,384]{2,1,0:T(8,128)(2,1)} %bitcast.34, ...), kind=kOutput, calls=%fused_computation.13 | convolution fusion | flops 1142046720 | bytes 22141440 | tf_op jit(solution)/shard_map/bik,bkr->bir/dot_general | solution.py:64
  51.1 3.5 %collective-permute-start.4 = (bf16[4,96,384]{2,1,0:T(8,128)(2,1)S(1)}, bf16[4,96,384]{2,1,0:T(8,128)(2,1)S(1)}, u32[]{:S(2)}, u32[]{:S(2)}) collective-permute-start(bf16[4,96,384]{2,1,0:T(8,128)(2,1)S(1)} %get-tuple-element.5), channel_id=1, source_target_pairs={{0,13},{1,0},{4,1},{5,4},{8,5},{9,8},{12,9},{13,12},{2,15},{3,2},{... | collective-permute-start | bytes 884744 | tf_op jit(solution)/shard_map/ppermute | solution.py:33
  54.6 6.9 %collective-permute-done.3 = bf16[4,96,384]{2,1,0:T(8,128)(2,1)S(1)} collective-permute-done((bf16[4,96,384]{2,1,0:T(8,128)(2,1)S(1)}, bf16[4,96,384]{2,1,0:T(8,128)(2,1)S(1)}, u32[]{:S(2)}, u32[]{:S(2)}) %collective-permute-start.3) | collective-permute-done | bytes 294944 | tf_op jit(solution)/shard_map/ppermute | solution.py:33
  61.5 1.6 %pad_maximum_fusion.1 = bf16[28,96,384]{2,1,0:T(8,128)(2,1)} fusion(bf16[4,96,384]{2,1,0:T(8,128)(2,1)S(1)} %collective-permute-done.4, bf16[20,96,384]{2,1,0:T(8,128)(2,1)S(1)} %get-tuple-element.24, bf16[4,96,384]{2,1,0:T(8,128)(2,1)S(1)} %collective-permute-done.3), kind=kLoop, calls=%fused_computation.15 | loop fusion | flops 2064384 | bytes 4128768 | tf_op jit(solution)/shard_map/concatenate | solution.py:62
  63.1 10.3 %gather_fusion.1 = bf16[160,96,384]{2,1,0:T(8,128)(2,1)} fusion(bf16[28,96,384]{2,1,0:T(8,128)(2,1)} %pad_maximum_fusion.1, s32[1024]{0:T(1024)S(1)} %pad_clamp_fusion), kind=kCustom, calls=%fused_computation.1 | custom fusion | bytes 23593600 | tf_op jit(solution)/shard_map/gather | solution.py:63
  73.4 10.4 %multiply_convert_fusion = (bf16[20,96,384]{2,1,0:T(8,128)(2,1)S(1)}, f32[20,96,384]{2,1,0:T(8,128)}) fusion(f32[20,96]{1,0:T(8,128)S(1)} %copy-done.4, f32[20,96,384]{2,1,0:T(8,128)} %get-tuple-element.25, bf16[20,96,384]{2,1,0:T(8,128)(2,1)} %param.9, bf16[20,96,384]{2,1,0:T(8,128)(2,1)} %copy-done.1, f32[20,96]{1,0:T(8,128)S(1)} %copy-done.5, ...), kind=kOutput, calls=%fused_computation.12 | convolution fusion | flops 1142784000 | bytes 25082880 | tf_op jit(solution)/shard_map/bik,bkr->bir/dot_general | solution.py:64
  83.9 3.5 %collective-permute-start.7 = (bf16[4,96,384]{2,1,0:T(8,128)(2,1)S(1)}, bf16[4,96,384]{2,1,0:T(8,128)(2,1)S(1)}, u32[]{:S(2)}, u32[]{:S(2)}) collective-permute-start(bf16[4,96,384]{2,1,0:T(8,128)(2,1)S(1)} %get-tuple-element.3), channel_id=1, source_target_pairs={{0,13},{1,0},{4,1},{5,4},{8,5},{9,8},{12,9},{13,12},{2,15},{3,2},{... | collective-permute-start | bytes 884744 | tf_op jit(solution)/shard_map/ppermute | solution.py:33
  87.4 6.7 %collective-permute-done.6 = bf16[4,96,384]{2,1,0:T(8,128)(2,1)S(1)} collective-permute-done((bf16[4,96,384]{2,1,0:T(8,128)(2,1)S(1)}, bf16[4,96,384]{2,1,0:T(8,128)(2,1)S(1)}, u32[]{:S(2)}, u32[]{:S(2)}) %collective-permute-start.6) | collective-permute-done | bytes 294944 | tf_op jit(solution)/shard_map/ppermute | solution.py:33
  94.1 1.6 %pad_maximum_fusion.2 = bf16[28,96,384]{2,1,0:T(8,128)(2,1)} fusion(bf16[4,96,384]{2,1,0:T(8,128)(2,1)S(1)} %collective-permute-done.7, bf16[20,96,384]{2,1,0:T(8,128)(2,1)S(1)} %get-tuple-element.26, bf16[4,96,384]{2,1,0:T(8,128)(2,1)S(1)} %collective-permute-done.6), kind=kLoop, calls=%fused_computation.16 | loop fusion | flops 2064384 | bytes 4128768 | tf_op jit(solution)/shard_map/concatenate | solution.py:62
  95.8 10.3 %gather_fusion.2 = bf16[160,96,384]{2,1,0:T(8,128)(2,1)} fusion(bf16[28,96,384]{2,1,0:T(8,128)(2,1)} %pad_maximum_fusion.2, s32[1024]{0:T(1024)S(1)} %pad_clamp_fusion), kind=kCustom, calls=%fused_computation.2 | custom fusion | bytes 23593600 | tf_op jit(solution)/shard_map/gather | solution.py:63
  106.0 11.8 %fusion.5 = (f32[20,96,384]{2,1,0:T(8,128)}, f32[20,96,384]{2,1,0:T(8,128)}) fusion(f32[20,96,384]{2,1,0:T(8,128)} %get-tuple-element.27, f32[20,96,384]{2,1,0:T(8,128)} %get-tuple-element.25, bf16[20,96,384]{2,1,0:T(8,128)(2,1)} %param.9, bf16[20,96,384]{2,1,0:T(8,128)(2,1)} %copy-done.2, f32[20,96]{1,0:T(8,128)S(1)} %copy-done.7, ...), kind=kOutput, calls=%fused_computation.18 | convolution fusion | flops 1138360320 | bytes 29498880 | tf_op jit(solution)/shard_map/bik,bkr->bir/dot_general | solution.py:64
  (44 shorter events, 9.7 us)
Async XLA Ops:
  0.6 42.7 %copy-start = (bf16[20,96,768]{2,1,0:T(8,128)(2,1)S(1)}, bf16[20,96,768]{2,1,0:T(8,128)(2,1)}, u32[]{:S(2)}) copy-start(bf16[20,96,768]{2,1,0:T(8,128)(2,1)} %param.10) | copy-start | bytes 8847364
  0.6 12.4 %copy-start.8 = (s32[3,20]{1,0:T(4,128)S(1)}, s32[3,20]{1,0:T(4,128)}, u32[]{:S(2)}) copy-start(s32[3,20]{1,0:T(4,128)} %param.14) | copy-start | bytes 724
  2.1 14.9 %collective-permute-start.8 = (f32[1,20,48]{2,1,0:T(8,128)}, f32[1,20,48]{2,1,0:T(8,128)}, u32[]{:S(2)}, u32[]{:S(2)}) collective-permute-start(f32[1,20,48]{2,1,0:T(8,128)} %slice.47), channel_id=1, source_target_pairs={{0,2},{2,0},{1,3},{3,1},{4,6},{6,4},{5,7},{7,5},{8,10},{10,8},{9,1... | collective-permute-start | bytes 11528 | tf_op jit(solution)/shard_map/ppermute | solution.py:20
  7.5 1.1 copy-start.3
  9.5 20.7 %collective-permute-start = (bf16[4,96,384]{2,1,0:T(8,128)(2,1)}, bf16[4,96,384]{2,1,0:T(8,128)(2,1)S(1)}, u32[]{:S(2)}, u32[]{:S(2)}) collective-permute-start(bf16[4,96,384]{2,1,0:T(8,128)(2,1)} %get-tuple-element.6), channel_id=1, source_target_pairs={{0,1},{1,4},{4,5},{5,8},{8,9},{9,12},{12,13},{13,0},{2,3},{3,6},{6... | collective-permute-start | bytes 884744 | tf_op jit(solution)/shard_map/ppermute | solution.py:33
  9.5 20.7 %collective-permute-start.1 = (bf16[4,96,384]{2,1,0:T(8,128)(2,1)}, bf16[4,96,384]{2,1,0:T(8,128)(2,1)S(1)}, u32[]{:S(2)}, u32[]{:S(2)}) collective-permute-start(bf16[4,96,384]{2,1,0:T(8,128)(2,1)} %get-tuple-element.7), channel_id=1, source_target_pairs={{0,13},{1,0},{4,1},{5,4},{8,5},{9,8},{12,9},{13,12},{2,15},{3,2},{... | collective-permute-start | bytes 884744 | tf_op jit(solution)/shard_map/ppermute | solution.py:33
  18.4 4.0 %collective-permute-start.2 = (f32[1,20,48]{2,1,0:T(8,128)}, f32[1,20,48]{2,1,0:T(8,128)}, u32[]{:S(2)}, u32[]{:S(2)}) collective-permute-start(f32[1,20,48]{2,1,0:T(8,128)} %get-tuple-element.14), channel_id=1, source_target_pairs={{0,2},{2,0},{1,3},{3,1},{4,6},{6,4},{5,7},{7,5},{8,10},{10,8},{9,1... | collective-permute-start | bytes 11528 | tf_op jit(solution)/shard_map/ppermute | solution.py:20
  18.4 4.1 %collective-permute-start.5 = (f32[1,20,48]{2,1,0:T(8,128)}, f32[1,20,48]{2,1,0:T(8,128)}, u32[]{:S(2)}, u32[]{:S(2)}) collective-permute-start(f32[1,20,48]{2,1,0:T(8,128)} %get-tuple-element.15), channel_id=1, source_target_pairs={{0,2},{2,0},{1,3},{3,1},{4,6},{6,4},{5,7},{7,5},{8,10},{10,8},{9,1... | collective-permute-start | bytes 11528 | tf_op jit(solution)/shard_map/ppermute | solution.py:20
  33.1 10.3 %copy-start.4 = (f32[20,96]{1,0:T(8,128)S(1)}, f32[20,96]{1,0:T(8,128)}, u32[]{:S(2)}) copy-start(f32[20,96]{1,0:T(8,128)} %param.12) | copy-start | bytes 23044
  33.1 10.3 %copy-start.6 = (f32[20,96]{1,0:T(8,128)S(1)}, f32[20,96]{1,0:T(8,128)}, u32[]{:S(2)}) copy-start(f32[20,96]{1,0:T(8,128)} %get-tuple-element.19) | copy-start | bytes 23044
  50.9 10.6 %copy-start.1 = (bf16[20,96,384]{2,1,0:T(8,128)(2,1)}, bf16[20,96,384]{2,1,0:T(8,128)(2,1)S(1)}, u32[]{:S(2)}) copy-start(bf16[20,96,384]{2,1,0:T(8,128)(2,1)S(1)} %get-tuple-element.24) | copy-start | bytes 4423684
  51.0 10.5 %collective-permute-start.3 = (bf16[4,96,384]{2,1,0:T(8,128)(2,1)S(1)}, bf16[4,96,384]{2,1,0:T(8,128)(2,1)S(1)}, u32[]{:S(2)}, u32[]{:S(2)}) collective-permute-start(bf16[4,96,384]{2,1,0:T(8,128)(2,1)S(1)} %get-tuple-element.4), channel_id=1, source_target_pairs={{0,1},{1,4},{4,5},{5,8},{8,9},{9,12},{12,13},{13,0},{2,3},{3,6},{6... | collective-permute-start | bytes 884744 | tf_op jit(solution)/shard_map/ppermute | solution.py:33
  51.1 10.4 %collective-permute-start.4 = (bf16[4,96,384]{2,1,0:T(8,128)(2,1)S(1)}, bf16[4,96,384]{2,1,0:T(8,128)(2,1)S(1)}, u32[]{:S(2)}, u32[]{:S(2)}) collective-permute-start(bf16[4,96,384]{2,1,0:T(8,128)(2,1)S(1)} %get-tuple-element.5), channel_id=1, source_target_pairs={{0,13},{1,0},{4,1},{5,4},{8,5},{9,8},{12,9},{13,12},{2,15},{3,2},{... | collective-permute-start | bytes 884744 | tf_op jit(solution)/shard_map/ppermute | solution.py:33
  63.1 10.3 %copy-start.5 = (f32[20,96]{1,0:T(8,128)S(1)}, f32[20,96]{1,0:T(8,128)}, u32[]{:S(2)}) copy-start(f32[20,96]{1,0:T(8,128)} %get-tuple-element.20) | copy-start | bytes 23044
  83.8 10.3 %copy-start.2 = (bf16[20,96,384]{2,1,0:T(8,128)(2,1)}, bf16[20,96,384]{2,1,0:T(8,128)(2,1)S(1)}, u32[]{:S(2)}) copy-start(bf16[20,96,384]{2,1,0:T(8,128)(2,1)S(1)} %get-tuple-element.26) | copy-start | bytes 4423684
  83.8 10.3 %collective-permute-start.6 = (bf16[4,96,384]{2,1,0:T(8,128)(2,1)S(1)}, bf16[4,96,384]{2,1,0:T(8,128)(2,1)S(1)}, u32[]{:S(2)}, u32[]{:S(2)}) collective-permute-start(bf16[4,96,384]{2,1,0:T(8,128)(2,1)S(1)} %get-tuple-element.2), channel_id=1, source_target_pairs={{0,1},{1,4},{4,5},{5,8},{8,9},{9,12},{12,13},{13,0},{2,3},{3,6},{6... | collective-permute-start | bytes 884744 | tf_op jit(solution)/shard_map/ppermute | solution.py:33
  83.9 10.2 %collective-permute-start.7 = (bf16[4,96,384]{2,1,0:T(8,128)(2,1)S(1)}, bf16[4,96,384]{2,1,0:T(8,128)(2,1)S(1)}, u32[]{:S(2)}, u32[]{:S(2)}) collective-permute-start(bf16[4,96,384]{2,1,0:T(8,128)(2,1)S(1)} %get-tuple-element.3), channel_id=1, source_target_pairs={{0,13},{1,0},{4,1},{5,4},{8,5},{9,8},{12,9},{13,12},{2,15},{3,2},{... | collective-permute-start | bytes 884744 | tf_op jit(solution)/shard_map/ppermute | solution.py:33
  95.8 10.3 %copy-start.7 = (f32[20,96]{1,0:T(8,128)S(1)}, f32[20,96]{1,0:T(8,128)}, u32[]{:S(2)}) copy-start(f32[20,96]{1,0:T(8,128)} %get-tuple-element.18) | copy-start | bytes 23044
